TPU v7x, 32 devices: a whole 2x2x4 slice. The times are simulated.
32 devices in a mesh: frame: 8 (over z, core), head: 4 (over y, x).
Axes of the slice: x: 2, y: 2, z: 4, core: 2. Of those that a mesh axis runs over, the one named last changes fastest.
Arguments:
- queries: bfloat16 [4096, 1024], P('frame', 'head'), may hold values from -6 to 6
- key_rows: bfloat16 [4096, 1024], P('frame', 'head'), may hold values from -6 to 6
- values: bfloat16 [4096, 1024], P('frame', 'head'), may hold values from -6 to 6
- gate_init: float32 [8, 128, 128], P('head'), may hold values from -0.5 to 0.5
- up_init: float32 [8, 128, 128], P('head'), may hold values from -0.5 to 0.5
- down_init: float32 [8, 128, 128], P('head'), may hold values from -0.5 to 0.5
- step_size: float32 [8], P('head'), may hold values from 0.1 to 1
- head_scale: float32 [8], P('head'), may hold values from 0.25 to 4
- out_gain: float32 [1024], P('head'), may hold values from 0.5 to 1.5
Outputs:
- layer_out: bfloat16 [4096, 1024], P('frame', 'head')
All inputs are finite; a program needn't handle non-finite values.
Results may differ from a plain program's by a relative error of at most 0.012.
The roundings to bfloat16 on the way count: a program that leaves them out, or rounds other values in their place, can miss the bound.
Values may be sent and summed in bfloat16 or wider, within the bound.
A program may use at most 64 MiB of HBM per device.

v0:
```python
import math

import jax
import jax.numpy as jnp
from jax import lax
from jax.sharding import PartitionSpec as P

NS_ITERS = 5
GROUPS = 2


quintic_terms = (3.4445, -4.775, 2.0315)
highest = lax.Precision.HIGHEST


def from_behind(block, axis, distance):
    devices = range(lax.axis_size(axis))
    route = [(i - distance, i) for i in devices if i - distance in devices]
    return lax.ppermute(block, axis, route)


def rms_scale(rows_in, epsilon):
    mean_square = jnp.mean(rows_in * rows_in, axis=-1, keepdims=True)
    return rows_in * lax.rsqrt(mean_square + epsilon)


def newton_schulz(gradient):
    flipped = gradient.shape[1] > gradient.shape[2]
    matrix = gradient
    frobenius = jnp.sqrt(jnp.sum(matrix * matrix, axis=(1, 2), keepdims=True))
    matrix = matrix / (frobenius + 1e-07)
    for repeat_no in range(NS_ITERS):
        square = jnp.einsum("hij,hkj->hik", matrix, matrix, precision=highest)
        quartic = jnp.einsum("hij,hjk->hik", square, square, precision=highest)
        mixing = quintic_terms[1] * square + quintic_terms[2] * quartic
        matrix = quintic_terms[0] * matrix + jnp.einsum(
            "hij,hjk->hik", mixing, matrix, precision=highest
        )
    return matrix


def column_norms(weight):
    return jnp.sqrt(jnp.sum(weight * weight, axis=1, keepdims=True))


def fast_grads(weights, key_part, value_part):
    gate_w, up_w, down_w = weights
    key_f = key_part.astype(jnp.float32)
    value_f = value_part.astype(jnp.float32)
    gate = jnp.einsum("nhd,hdf->nhf", key_f, gate_w, precision=highest)
    upward = jnp.einsum("nhd,hdf->nhf", key_f, up_w, precision=highest)
    sigma = jax.nn.sigmoid(gate)
    active = gate * sigma
    hidden = active * upward
    back_hidden = -jnp.einsum("nhd,hfd->nhf", value_f, down_w, precision=highest)
    grad_down = -jnp.einsum("nhf,nhd->hfd", hidden, value_f, precision=highest)
    back_gate = back_hidden * upward * sigma * (1.0 + gate * (1.0 - sigma))
    back_up = back_hidden * active
    grad_gate = jnp.einsum("nhd,nhf->hdf", key_f, back_gate, precision=highest)
    grad_up = jnp.einsum("nhd,nhf->hdf", key_f, back_up, precision=highest)
    return (grad_gate, grad_up, grad_down)


def summed(gradients):
    return lax.psum((gradients[0], gradients[1], gradients[2]), "frame")


def orthogonal(gradients):
    return tuple((newton_schulz(gradient) for gradient in gradients))


def renewed(weights, gradients, step_size, targets):
    result = []
    for weight, ortho, target in zip(weights, orthogonal(gradients), targets):
        moved = weight - step_size[:, None, None] * ortho
        length = jnp.sqrt(jnp.sum(moved * moved, axis=1, keepdims=True))
        result.append(moved * (target / (length + 1e-06)))
    return tuple(result)


def fast_apply(weights, query_part, head_scale):
    gate_w, up_w, down_w = weights
    query_f = query_part.astype(jnp.float32)
    gate = jnp.einsum("nhd,hdf->nhf", query_f, gate_w, precision=highest)
    upward = jnp.einsum("nhd,hdf->nhf", query_f, up_w, precision=highest)
    hidden = jax.nn.silu(gate) * upward
    output = jnp.einsum("nhf,hfd->nhd", hidden, down_w, precision=highest)
    return (output * head_scale[None, :, None]).astype(jnp.bfloat16)


def attend(queries, keys_here, values_here, keys_prev, values_prev, is_first, heads_dev, head_dim):
    frame_len = queries.shape[0]
    score_scale = 1.0 / math.sqrt(head_dim)
    rows_per = frame_len
    while rows_per > 1024 and rows_per % 2 == 0:
        rows_per = rows_per // 2
    blocks = frame_len // rows_per
    column = lax.broadcasted_iota(jnp.int32, (1, 2 * frame_len), 1)
    masked = jnp.logical_and(is_first, column < frame_len)
    outputs = []
    for head_no in range(heads_dev):
        lower = head_no * head_dim
        upper = lower + head_dim
        key_all = jnp.concatenate([keys_prev[:, lower:upper], keys_here[:, lower:upper]], axis=0)
        value_all = jnp.concatenate(
            [values_prev[:, lower:upper], values_here[:, lower:upper]], axis=0
        )
        query_blocks = queries[:, lower:upper].reshape(blocks, rows_per, head_dim)

        def one_block(query_part):
            scores = (
                jnp.einsum("qd,kd->qk", query_part, key_all, preferred_element_type=jnp.float32)
                * score_scale
            )
            scores = jnp.where(masked, -1e30, scores)
            probs = jax.nn.softmax(scores, axis=-1).astype(jnp.bfloat16)
            mixed = jnp.dot(probs, value_all, preferred_element_type=jnp.float32)
            return rms_scale(mixed, 1e-06).astype(jnp.bfloat16)

        outputs.append(lax.map(one_block, query_blocks).reshape(frame_len, head_dim))
    return jnp.concatenate(outputs, axis=1)


def shards(
    queries, key_rows, values, gate_init, up_init, down_init, step_size, head_scale, out_gain
):
    frame_len, width = queries.shape
    heads_dev = gate_init.shape[0]
    head_dim = gate_init.shape[1]
    keys_prev, values_prev = from_behind((key_rows, values), "frame", 1)
    position = lax.axis_index("frame")
    attended = attend(
        queries, key_rows, values, keys_prev, values_prev, position == 0, heads_dev, head_dim
    )
    query_norm = rms_scale(
        queries.astype(jnp.float32).reshape(frame_len, heads_dev, head_dim), 1e-06
    ).astype(jnp.bfloat16)
    frames_count = lax.axis_size("frame")
    half = frames_count // GROUPS
    weights = (gate_init, up_init, down_init)
    targets = tuple((column_norms(weight) for weight in weights))
    segment_mine = position // half
    key_view = attended.reshape(frame_len, heads_dev, head_dim)
    value_view = values.reshape(frame_len, heads_dev, head_dim)
    history = []
    for segment in range(GROUPS):
        current = weights
        local_terms = lax.cond(
            segment_mine == segment,
            lambda: fast_grads(current, key_view, value_view),
            lambda: tuple((jnp.zeros_like(weight) for weight in current)),
        )
        weights = renewed(weights, summed(local_terms), step_size, targets)
        history.append(weights)
    chosen = tuple(
        (jnp.stack([state[member] for state in history])[segment_mine] for member in range(3))
    )
    fast_out = fast_apply(chosen, query_norm, head_scale).reshape(frame_len, width)
    combined = attended.astype(jnp.float32) + fast_out.astype(jnp.float32)
    local_sum = jnp.sum(combined * combined, axis=1)
    total = lax.psum(local_sum, "head")
    features = width * lax.axis_size("head")
    scaled = combined * lax.rsqrt(total / features + 1e-05)[:, None] * out_gain[None, :]
    return scaled.astype(jnp.bfloat16)


def solution(mesh):
    in_specs = (
        P("frame", "head"),
        P("frame", "head"),
        P("frame", "head"),
        P("head", None, None),
        P("head", None, None),
        P("head", None, None),
        P("head"),
        P("head"),
        P("head"),
    )
    out_specs = P("frame", "head")
    return jax.shard_map(shards, mesh=mesh, in_specs=in_specs, out_specs=out_specs, check_vma=False)
```

profile of v0, /device:TPU:0, one launch (start us, length us, event | category | flops | bytes accessed | tf_op | source)
XLA Modules:
  0.0 199.2 jit_solution(9059717988215730369)
XLA Ops:
  6.5 2.5 %collective-permute-start = (bf16[512,256]{1,0:T(8,128)(2,1)}, bf16[512,256]{1,0:T(8,128)(2,1)S(1)}, u32[]{:S(2)}, u32[]{:S(2)}) collective-permute-start(bf16[512,256]{1,0:T(8,128)(2,1)} %param.14), channel_id=1, source_target_pairs={{0,4},{4,8},{8,12},{12,16},{16,20},{20,24},{24,28},{1,5},{5,9},{9,... | collective-permute-start | bytes 786440 | tf_op jit(solution)/shard_map/ppermute | solution.py:19
  9.1 4.6 %collective-permute-start.1 = (bf16[512,256]{1,0:T(8,128)(2,1)}, bf16[512,256]{1,0:T(8,128)(2,1)S(1)}, u32[]{:S(2)}, u32[]{:S(2)}) collective-permute-start(bf16[512,256]{1,0:T(8,128)(2,1)} %param.15), channel_id=1, source_target_pairs={{0,4},{4,8},{8,12},{12,16},{16,20},{20,24},{24,28},{1,5},{5,9},{9,... | collective-permute-start | bytes 786440 | tf_op jit(solution)/shard_map/ppermute | solution.py:19
  13.7 1.0 fusion.137
  14.7 0.9 multiply_reduce_fusion.13
  15.6 0.9 multiply_reduce_fusion.16
  16.5 0.9 multiply_reduce_fusion.10
  17.5 1.1 copy.124
  18.7 1.1 copy.112
  20.5 0.8 fusion.34
  21.3 0.5 fusion.35
  21.9 0.8 multiply_reduce_fusion.1
  22.7 0.8 multiply_reduce_fusion.2
  23.7 2.8 %conditional.2 = (f32[2,128,128]{1,2,0:T(8,128)S(1)}, f32[2,128,128]{1,2,0:T(8,128)S(1)}, f32[2,128,128]{2,1,0:T(8,128)S(1)}) conditional(s32[]{:T(128)} %convert_element_type.62, () %tuple.25, (f32[2,128,128]{2,1,0:T(8,128)S(1)}, bf16[512,2,128]{0,2,1:T(8,128)(2,1)S(1)}, f32[2,128,128]{2,1,0:T(8,128)S(1)}, bf16[512,2,128]{0,2,1:T(8,128)(2,1)S(1)}, ...), branch_computations={%region_6.7_spmd, %region_7.8_spmd} | conditional | flops 1210613760 | bytes 7602200 | solution.py:148
  25.0 0.6 convolution_bitcast_fusion.3
  25.5 0.5 convolution_bitcast_fusion.2
  26.5 0.8 copy.117
  27.3 0.8 copy.118
  28.3 55.2 %all-reduce.7.cloned.1.call-done = (f32[2,128,128]{2,1,0:T(8,128)}, f32[2,128,128]{2,1,0:T(8,128)}, f32[2,128,128]{2,1,0:T(8,128)}) async-done(((f32[2,128,128]{2,1,0:T(8,128)}, f32[2,128,128]{2,1,0:T(8,128)}, f32[2,128,128]{2,1,0:T(8,128)}), (f32[2,128,128]{2,1,0:T(8,128)}, f32[2,128,128]{2,1,0:T(8,128)}, f32[2,128,128]{2,1,0:T(8,128)})) %all-reduce.7.cloned.1.call-update) | async-done | bytes 393232 | tf_op jit(solution)/shard_map/psum | solution.py:65
  83.5 1.0 multiply_reduce_fusion.17
  84.6 1.5 fusion.113
  86.3 1.3 convolution_add_fusion.29
  101.9 0.8 copy.123
  102.7 0.8 copy.129
  103.5 58.0 %all-reduce.5.cloned.1.call-done = (f32[2,128,128]{2,1,0:T(8,128)}, f32[2,128,128]{2,1,0:T(8,128)}, f32[2,128,128]{2,1,0:T(8,128)}) async-done(((f32[2,128,128]{2,1,0:T(8,128)}, f32[2,128,128]{2,1,0:T(8,128)}, f32[2,128,128]{2,1,0:T(8,128)}), (f32[2,128,128]{2,1,0:T(8,128)}, f32[2,128,128]{2,1,0:T(8,128)}, f32[2,128,128]{2,1,0:T(8,128)})) %all-reduce.5.cloned.1.call-update) | async-done | bytes 393232 | tf_op jit(solution)/shard_map/psum | solution.py:65
  161.5 1.0 multiply_reduce_fusion.8
  162.5 1.5 fusion.116
  164.3 1.3 convolution_add_fusion.14
  179.6 0.6 convolution_bitcast_fusion.9
  180.2 0.6 fusion.36
  180.9 0.7 fusion.87
  181.6 9.8 %psum.55 = f32[512]{0:T(512)S(1)} all-reduce(f32[512]{0:T(512)S(1)} %get-tuple-element.214), channel_id=1, replica_groups=mesh['frame'=8,'head'=4] {'head'}, use_global_device_ids=true, to_apply=%region_33.34 | all-reduce | flops 512 | bytes 4096 | tf_op jit(solution)/shard_map/psum | solution.py:161
  191.5 0.8 copy.133
  (169 shorter events, 31.3 us)
Async XLA Ops:
  6.5 13.4 %copy-start.3 = (bf16[512,256]{1,0:T(8,128)(2,1)S(1)}, bf16[512,256]{1,0:T(8,128)(2,1)}, u32[]{:S(2)}) copy-start(bf16[512,256]{1,0:T(8,128)(2,1)} %param.15) | copy-start | bytes 786436
  6.5 13.5 %copy-start.6 = (bf16[512,256]{1,0:T(8,128)(2,1)S(1)}, bf16[512,256]{1,0:T(8,128)(2,1)}, u32[]{:S(2)}) copy-start(bf16[512,256]{1,0:T(8,128)(2,1)} %param.13) | copy-start | bytes 786436
  6.5 77.0 %all-reduce.7.cloned.1.call-start = ((), (), s32[]{:S(2)}) async-start(), calls=%async_computation.1 | async-start | bytes 786432 | tf_op jit(solution)/shard_map/psum | solution.py:65
  6.5 13.5 %collective-permute-start = (bf16[512,256]{1,0:T(8,128)(2,1)}, bf16[512,256]{1,0:T(8,128)(2,1)S(1)}, u32[]{:S(2)}, u32[]{:S(2)}) collective-permute-start(bf16[512,256]{1,0:T(8,128)(2,1)} %param.14), channel_id=1, source_target_pairs={{0,4},{4,8},{8,12},{12,16},{16,20},{20,24},{24,28},{1,5},{5,9},{9,... | collective-permute-start | bytes 786440 | tf_op jit(solution)/shard_map/ppermute | solution.py:19
  9.1 12.7 %collective-permute-start.1 = (bf16[512,256]{1,0:T(8,128)(2,1)}, bf16[512,256]{1,0:T(8,128)(2,1)S(1)}, u32[]{:S(2)}, u32[]{:S(2)}) collective-permute-start(bf16[512,256]{1,0:T(8,128)(2,1)} %param.15), channel_id=1, source_target_pairs={{0,4},{4,8},{8,12},{12,16},{16,20},{20,24},{24,28},{1,5},{5,9},{9,... | collective-permute-start | bytes 786440 | tf_op jit(solution)/shard_map/ppermute | solution.py:19
  22.7 0.9 copy-start
  22.7 1.0 copy-start.1
  22.7 1.0 copy-start.2
  26.5 1.5 copy-start.4
  28.1 133.4 %all-reduce.5.cloned.1.call-start = ((), (), s32[]{:S(2)}) async-start(), calls=%async_computation | async-start | bytes 786432 | tf_op jit(solution)/shard_map/psum | solution.py:65
  87.6 3.5 %copy-start.11 = (f32[2]{0:T(128)S(1)}, f32[2]{0:T(128)}, u32[]{:S(2)}) copy-start(f32[2]{0:T(128)} %param.19) | copy-start | bytes 28
  88.6 3.0 %copy-start.7 = (f32[2,128,128]{2,1,0:T(8,128)S(1)}, f32[2,128,128]{2,1,0:T(8,128)}, u32[]{:S(2)}) copy-start(f32[2,128,128]{2,1,0:T(8,128)} %get-tuple-element.184) | copy-start | bytes 393220
  88.6 3.0 %copy-start.9 = (f32[2,128,128]{2,1,0:T(8,128)S(1)}, f32[2,128,128]{2,1,0:T(8,128)}, u32[]{:S(2)}) copy-start(f32[2,128,128]{2,1,0:T(8,128)} %get-tuple-element.186) | copy-start | bytes 393220
  101.9 1.5 copy-start.5
  166.3 3.2 %copy-start.10 = (f32[2,128,128]{2,1,0:T(8,128)S(1)}, f32[2,128,128]{2,1,0:T(8,128)}, u32[]{:S(2)}) copy-start(f32[2,128,128]{2,1,0:T(8,128)} %get-tuple-element.182) | copy-start | bytes 393220
  171.3 3.2 %copy-start.8 = (f32[2,128,128]{2,1,0:T(8,128)S(1)}, f32[2,128,128]{2,1,0:T(8,128)}, u32[]{:S(2)}) copy-start(f32[2,128,128]{2,1,0:T(8,128)} %get-tuple-element.181) | copy-start | bytes 393220
  179.6 1.2 copy-start.13
  180.2 11.2 %copy-start.12 = (f32[256]{0:T(256)S(1)}, f32[256]{0:T(256)}, u32[]{:S(2)}) copy-start(f32[256]{0:T(256)} %param.21) | copy-start | bytes 3076
Sparse Core Ops, SparseCore 0:
  28.2 55.2 all-reduce.6
  103.6 57.8 all-reduce.4
where the time goes:
time: 200 us; the launch traced here: 199 us
  waiting for transfers between devices  113 us (56%)
  matrix products  40.2 us (20%)
  between operations  14.5 us (7%)
  blocking collectives  9.84 us (5%)
  local copies, waits for them, and re-layouts  7.46 us (4%)
  starting transfers between devices  7.34 us (4%)
  other arithmetic  6.28 us (3%)
    psum x2, waiting for transfers between devices, summed(): return lax.psum((gradients[0], gradients[1], gradients[2]), 'frame')  113 us
    dot_general x30, matrix products, newton_schulz(): square = jnp.einsum('hij,hkj->hik', matrix, matrix, precision=highest)  14 us
    dot_general x30, matrix products, newton_schulz(): jnp.einsum('hij,hjk->hik', mixing, matrix, precision=highest)  10.6 us
    psum x1, blocking collectives, shards(): total = lax.psum(local_sum, 'head')  9.84 us
    dot_general x30, matrix products, newton_schulz(): quartic = jnp.einsum('hij,hjk->hik', square, square, precision=highest)  8.14 us
    ppermute x2, starting transfers between devices, from_behind(): return lax.ppermute(block, axis, route)  7.12 us
  transfers between devices with their start and end apart: 4, of which 2 were waited for; matrix products, arithmetic and copies ran while one was open for 4% of the time, Pallas kernels for 0%

commit v1 on v0

v1 whole, which is shorter than its diff:
```python
import functools
import math

import jax
import jax.numpy as jnp
from jax import lax
from jax.experimental import pallas as pl
from jax.experimental.pallas import tpu as pltpu
from jax.sharding import PartitionSpec as P

NS_ITERS = 5
GROUPS = 2
MESH = pl.DeviceIdType.MESH
SENT = jnp.bfloat16
COARSE = 2
BF = jnp.bfloat16
F32 = jnp.float32
quintic_terms = (3.4445, -4.775, 2.0315)


def dot_nt(a, b):
    return lax.dot_general(a, b, (((1,), (1,)), ((), ())), preferred_element_type=F32)


def dot_nn(a, b):
    return lax.dot_general(a, b, (((1,), (0,)), ((), ())), preferred_element_type=F32)


def dot_tn(a, b):
    return lax.dot_general(a, b, (((0,), (0,)), ((), ())), preferred_element_type=F32)


def split(x):
    high = x.astype(BF)
    return high, (x - high.astype(F32)).astype(BF)


def side(*parts):
    return jnp.concatenate(parts, axis=1)


def over(*parts):
    return jnp.concatenate(parts, axis=0)


def sigmoid(v):
    return 0.5 * (1.0 + jnp.tanh(0.5 * v))


def parts_of(x, fine):
    return split(x) if fine else (x.astype(BF),)


def left(parts):
    return side(parts[0], parts[1], parts[0]) if len(parts) == 2 else parts[0]


def right(parts, axis):
    if len(parts) == 1:
        return parts[0]
    return jnp.concatenate((parts[0], parts[0], parts[1]), axis=axis)


def newton_schulz(grads):
    xs = []
    for m in grads:
        norm = jnp.sqrt(jnp.sum(m * m, keepdims=True))
        xs.append(m * (1.0 / (norm + 1e-07)))
    for step in range(NS_ITERS):
        fine = step >= COARSE
        halves = [parts_of(x, fine) for x in xs]
        squares = [dot_nt(left(h), right(h, 1)) for h in halves]
        sq = [parts_of(a, fine) for a in squares]
        quartics = [dot_nn(left(a), right(a, 0)) for a in sq]
        mixing = [quintic_terms[1] * a + quintic_terms[2] * q for a, q in zip(squares, quartics)]
        xs = [
            quintic_terms[0] * x + dot_nn(left(parts_of(b, fine)), right(h, 0))
            for x, b, h in zip(xs, mixing, halves)
        ]
    return xs


def lengths(m, axis):
    return jnp.sqrt(jnp.sum(m * m, axis=axis, keepdims=True))


AXES = (1, 1, 0)


def kernel(
    dims,
    q_any, k_any, v_any, gate_any, up_any, down_any, gain_ref, step_ref, scale_ref,
    out_ref,
    q_ref, k_ref, v_ref, gate_ref, up_ref, down_ref, local_sem,
    kp, vp, here, before, mix, top, den, att, qn, comb, wb, wf, target, gp, rp, cs, rz, tot, fw, part, others,
    kv_send, kv_recv, pair_send, pair_recv, mate_send, mate_recv, fw_send, fw_recv,
    w_send, w_recv, head_send, head_recv,
):
    frames, nh, hd = dims
    rows, width = q_any.shape
    dh = width // hd
    half = frames // GROUPS
    mates = half // 2
    own = hd // 2
    p = lax.axis_index("frame")
    j = lax.axis_index("head")
    core = lax.rem(p, 2)
    seg = p // half
    rank = lax.rem(p, half) // 2
    pair = p + 1 - 2 * core
    has_prev = p > 0
    has_next = p < frames - 1
    prev_far = jnp.logical_and(core == 0, has_prev)
    next_far = jnp.logical_and(core == 1, has_next)

    locals_ = [
        pltpu.make_async_copy(src, dst, local_sem.at[n])
        for n, (src, dst) in enumerate(
            zip(
                (k_any, q_any, v_any, gate_any, up_any, down_any),
                (k_ref, q_ref, v_ref, gate_ref, up_ref, down_ref),
            )
        )
    ]

    def start_local():
        for copy in locals_:
            copy.start()

    def fw_targets(s):
        return [(to, r) for to in reversed(range(s + 1, GROUPS)) for r in reversed(range(mates))]

    barrier = pltpu.get_barrier_semaphore()

    def greet(frame_at, head_at):
        pl.semaphore_signal(barrier, inc=1, device_id=(frame_at, head_at), device_id_type=MESH)

    greet(pair, j)

    @pl.when(next_far)
    def _():
        greet(p + 1, j)

    @pl.when(prev_far)
    def _():
        greet(p - 1, j)

    def mate_at(step):
        return seg * half + 2 * lax.rem(rank + step, mates) + core

    def head_at(step):
        return lax.rem(j + step, nh)

    for step in range(1, mates):
        greet(mate_at(step), j)
    for step in range(1, nh):
        greet(p, head_at(step))
    is_last = rank == mates - 1
    for s in range(GROUPS):
        @pl.when(jnp.logical_and(is_last, seg == s))
        def _(s=s):
            for to, r in fw_targets(s):
                greet(to * half + 2 * r + core, j)

        @pl.when(seg > s)
        def _(s=s):
            greet(s * half + 2 * (mates - 1) + core, j)

    start_local()
    count = mates - 1 + nh - 1 + 1 + seg
    far = prev_far.astype(jnp.int32) + next_far.astype(jnp.int32)
    far = far + is_last.astype(jnp.int32) * (GROUPS - 1 - seg) * mates
    pl.semaphore_wait(barrier, count + far)

    ahead = jnp.minimum(p + 1, frames - 1)

    def kv_copy(h, which):
        src, dst = ((k_any, kp), (v_any, vp))[which]
        return pltpu.make_async_remote_copy(
            src_ref=src.at[:, pl.ds(h * dh, dh)],
            dst_ref=dst.at[h],
            send_sem=kv_send.at[2 * h + which],
            recv_sem=kv_recv.at[2 * h + which],
            device_id=(ahead, j),
            device_id_type=MESH,
        )

    @pl.when(has_next)
    def _():
        for which in range(2):
            for h in range(hd):
                kv_copy(h, which).start()

    factor = math.log2(math.e) / math.sqrt(dh)

    block = min(rows, 256)

    for copy in locals_:
        copy.wait()

    def exps(q, keys):
        scores = dot_nt(q, keys) * factor
        high = jnp.max(scores, axis=1, keepdims=True)
        e = jnp.exp2(scores - high)
        return e, high, jnp.sum(e, axis=1, keepdims=True)

    for h in range(hd):
        cols = slice(h * dh, (h + 1) * dh)
        for r in range(0, rows, block):
            rs = slice(r, r + block)
            e, t, d = exps(q_ref[rs, cols], k_ref[:, cols])
            here[h, rs] = e
            top[h, rs] = t
            den[h, rs] = d
        qf = q_ref[:, cols].astype(F32)
        mean = jnp.mean(qf * qf, axis=1, keepdims=True)
        qn[h] = (qf * lax.rsqrt(mean + 1e-06)).astype(BF)
        for m, ref in enumerate((gate_ref, up_ref, down_ref)):
            w = ref[h]
            w = w.T if AXES[m] else w
            high, low = split(w)
            wb[0, h, m] = side(high, low)
    for i in range(own):
        h = core * own + i
        for m, ref in enumerate((gate_ref, up_ref, down_ref)):
            w = ref[h]
            w = w.T if AXES[m] else w
            wf[i, m] = w
            target[i, m] = jnp.broadcast_to(lengths(w, AXES[m]), w.shape)

    @pl.when(has_prev)
    def _():
        for h in range(hd):
            cols = slice(h * dh, (h + 1) * dh)
            kv_copy(h, 0).wait_recv()
            for r in range(0, rows, block):
                rs = slice(r, r + block)
                e, t, d = exps(q_ref[rs, cols], kp[h])
                t0 = top[h, rs]
                high = jnp.maximum(t, t0)
                a, b = jnp.exp2(t0 - high), jnp.exp2(t - high)
                inv = 1.0 / (den[h, rs] * a + d * b)
                before[h, rs] = (e * (b * inv)).astype(BF)
                probs = (here[h, rs] * (a * inv)).astype(BF)
                mix[h, rs] = dot_nn(probs, v_ref[:, cols])

    @pl.when(jnp.logical_not(has_prev))
    def _():
        for h in range(hd):
            cols = slice(h * dh, (h + 1) * dh)
            for r in range(0, rows, block):
                rs = slice(r, r + block)
                probs = (here[h, rs] * (1.0 / den[h, rs])).astype(BF)
                mix[h, rs] = dot_nn(probs, v_ref[:, cols])

    for h in range(hd):
        @pl.when(has_prev)
        def _(h=h):
            kv_copy(h, 1).wait_recv()
            mix[h] = mix[h] + dot_nn(before[h], vp[h])

        m = mix[h]
        mean = jnp.mean(m * m, axis=1, keepdims=True)
        att[h] = (m * lax.rsqrt(mean + 1e-06)).astype(BF)

    def pair_copy(i, m):
        return pltpu.make_async_remote_copy(
            src_ref=gp.at[(1 - core) * own + i, m],
            dst_ref=rp.at[i, m],
            send_sem=pair_send.at[i * 3 + m],
            recv_sem=pair_recv.at[i * 3 + m],
            device_id=(pair, j),
            device_id_type=MESH,
        )

    def mate_copy(step, i, m):
        return pltpu.make_async_remote_copy(
            src_ref=cs.at[i, m],
            dst_ref=rz.at[step - 1, i, m],
            send_sem=mate_send.at[step - 1, i * 3 + m],
            recv_sem=mate_recv.at[step - 1, i * 3 + m],
            device_id=(mate_at(step), j),
            device_id_type=MESH,
        )

    def fw_copy(s, to, r, i, m):
        return pltpu.make_async_remote_copy(
            src_ref=cs.at[own + i, m],
            dst_ref=fw.at[s, i, m],
            send_sem=fw_send.at[(to - s - 1) * mates + r, i * 3 + m],
            recv_sem=fw_recv.at[s, i * 3 + m],
            device_id=(to * half + 2 * r + core, j),
            device_id_type=MESH,
        )

    def w_copy(state, i, m, which):
        at = which * own + i
        span = pl.ds(0, dh if state == GROUPS else 2 * dh)
        return pltpu.make_async_remote_copy(
            src_ref=wb.at[state, at, m, :, span],
            dst_ref=wb.at[state, at, m, :, span],
            send_sem=w_send.at[state - 1, i * 3 + m],
            recv_sem=w_recv.at[state - 1, i * 3 + m],
            device_id=(pair, j),
            device_id_type=MESH,
        )

    def fast_grads(state, h):
        x = att[h]
        y = v_ref[:, pl.ds(pl.multiple_of(h * dh, dh), dh)]
        xx = side(x, x)
        gate = dot_nt(wb[state, h, 0], xx)
        upward = dot_nt(wb[state, h, 1], xx)
        back = -dot_nt(wb[state, h, 2], side(y, y))
        sig = sigmoid(gate)
        active = gate * sig
        hidden = active * upward
        gp[h, 2] = -dot_nn(hidden.astype(BF), y)
        back_gate = back * upward * sig * (1.0 + gate * (1.0 - sig))
        gp[h, 0] = dot_nn(back_gate.astype(BF), x)
        gp[h, 1] = dot_nn((back * active).astype(BF), x)

    for s in range(GROUPS):
        @pl.when(seg == s)
        def _(s=s):
            for i in range(own):
                fast_grads(s, (1 - core) * own + i)
                for m in range(3):
                    pair_copy(i, m).start()
            for i in range(own):
                fast_grads(s, core * own + i)
            for i in range(own):
                for m in range(3):
                    pair_copy(i, m).wait_recv()
                    chip = gp[core * own + i, m] + rp[i, m]
                    cs[i, m] = chip.astype(SENT)
                    for step in range(1, mates):
                        mate_copy(step, i, m).start()
                    tot[i, m] = chip
            for i in range(own):
                for m in range(3):
                    total = tot[i, m]
                    for step in range(1, mates):
                        mate_copy(step, i, m).wait_recv()
                        total = total + rz[step - 1, i, m].astype(F32)
                    tot[i, m] = total
                    if s < GROUPS - 1:
                        cs[own + i, m] = total.astype(SENT)

                        @pl.when(rank == mates - 1)
                        def _(i=i, m=m):
                            fw_copy(s, *fw_targets(s)[0], i, m).start()

            if s < GROUPS - 1:
                @pl.when(rank == mates - 1)
                def _():
                    for to, r in fw_targets(s)[1:]:
                        for i in range(own):
                            for m in range(3):
                                fw_copy(s, to, r, i, m).start()

        if s < GROUPS - 1:
            @pl.when(seg > s)
            def _(s=s):
                for i in range(own):
                    for m in range(3):
                        fw_copy(s, s + 1, 0, i, m).wait_recv()
                        tot[i, m] = fw[s, i, m].astype(F32)

        @pl.when(seg >= s)
        def _(s=s):
            for i in range(own):
                at = core * own + i
                rate = step_ref[at]
                ortho = newton_schulz([tot[i, m] for m in range(3)])
                for m in range(3):
                    moved = wf[i, m] - rate * ortho[m]
                    w = moved * (target[i, m] / (lengths(moved, AXES[m]) + 1e-06))
                    if s < GROUPS - 1:
                        wf[i, m] = w
                    high, low = split(w)
                    wb[s + 1, at, m] = side(high, low)
                    w_copy(s + 1, i, m, core).start()
            for i in range(own):
                for m in range(3):
                    w_copy(s + 1, i, m, 1 - core).wait_recv()

    ones = jnp.ones((8, dh), BF)
    sums = jnp.zeros((8, rows), F32)
    mine = seg + 1
    for h in range(hd):
        cols = slice(h * dh, (h + 1) * dh)
        x = qn[h]
        gate = dot_nt(x, wb[mine, h, 0][:, :dh])
        upward = dot_nt(x, wb[mine, h, 1][:, :dh])
        hidden = (gate * sigmoid(gate) * upward).astype(BF)
        out = dot_nn(hidden, wb[mine, h, 2][:, :dh])
        fast = (out * scale_ref[h]).astype(BF)
        both = att[h].astype(F32) + fast.astype(F32)
        comb[:, cols] = both
        high, low = split(both * both)
        sums = sums + dot_nt(side(ones, ones), side(high, low))
    sums = jnp.maximum(sums, 0.0)
    part[...] = sums

    def head_copy(step):
        return pltpu.make_async_remote_copy(
            src_ref=part,
            dst_ref=others.at[step - 1],
            send_sem=head_send.at[step - 1],
            recv_sem=head_recv.at[step - 1],
            device_id=(p, head_at(step)),
            device_id_type=MESH,
        )

    for step in range(1, nh):
        head_copy(step).start()
    for step in range(1, nh):
        head_copy(step).wait_recv()
        sums = sums + others[step - 1]
    high, low = split(lax.rsqrt(sums / (width * nh) + 1e-05))
    eighths = jnp.full((16, dh), 0.125, BF)
    inverse = dot_tn(over(high.astype(F32), low.astype(F32)).astype(BF), eighths)
    for h in range(hd):
        cols = slice(h * dh, (h + 1) * dh)
        out_ref[:, cols] = comb[:, cols] * inverse

    for step in range(1, nh):
        head_copy(step).wait_send()

    @pl.when(has_next)
    def _():
        for h in range(hd):
            for which in range(2):
                kv_copy(h, which).wait_send()

    for i in range(own):
        for m in range(3):
            pair_copy(i, m).wait_send()
            for step in range(1, mates):
                mate_copy(step, i, m).wait_send()
    for s in range(GROUPS):
        @pl.when(seg >= s)
        def _(s=s):
            for i in range(own):
                for m in range(3):
                    w_copy(s + 1, i, m, core).wait_send()

        if s < GROUPS - 1:
            @pl.when(jnp.logical_and(seg == s, rank == mates - 1))
            def _(s=s):
                for to, r in fw_targets(s):
                    for i in range(own):
                        for m in range(3):
                            fw_copy(s, to, r, i, m).wait_send()


def shards(
    queries, key_rows, values, gate_init, up_init, down_init, step_size, head_scale, out_gain
):
    rows, width = queries.shape
    hd, dh, fwh = gate_init.shape
    frames, nh = lax.axis_size("frame"), lax.axis_size("head")
    mates = frames // GROUPS // 2
    own = hd // 2
    dma = pltpu.SemaphoreType.DMA
    vmem = pl.BlockSpec(memory_space=pltpu.VMEM)
    smem = pl.BlockSpec(memory_space=pltpu.SMEM)
    scaled = pl.pallas_call(
        functools.partial(kernel, (frames, nh, hd)),
        out_shape=jax.ShapeDtypeStruct((rows, width), F32),
        in_specs=[pl.BlockSpec(memory_space=pl.ANY)] * 6 + [vmem] + [smem] * 2,
        out_specs=vmem,
        scratch_shapes=[
            pltpu.VMEM((rows, width), BF),
            pltpu.VMEM((rows, width), BF),
            pltpu.VMEM((rows, width), BF),
            pltpu.VMEM((hd, dh, fwh), F32),
            pltpu.VMEM((hd, dh, fwh), F32),
            pltpu.VMEM((hd, fwh, dh), F32),
            dma((6,)),
            pltpu.VMEM((hd, rows, dh), BF),
            pltpu.VMEM((hd, rows, dh), BF),
            pltpu.VMEM((hd, rows, rows), F32),
            pltpu.VMEM((hd, rows, rows), BF),
            pltpu.VMEM((hd, rows, dh), F32),
            pltpu.VMEM((hd, rows, 1), F32),
            pltpu.VMEM((hd, rows, 1), F32),
            pltpu.VMEM((hd, rows, dh), BF),
            pltpu.VMEM((hd, rows, dh), BF),
            pltpu.VMEM((rows, width), F32),
            pltpu.VMEM((GROUPS + 1, hd, 3, dh, 2 * fwh), BF),
            pltpu.VMEM((own, 3, dh, fwh), F32),
            pltpu.VMEM((own, 3, dh, fwh), F32),
            pltpu.VMEM((hd, 3, dh, fwh), F32),
            pltpu.VMEM((own, 3, dh, fwh), F32),
            pltpu.VMEM((2 * own, 3, dh, fwh), SENT),
            pltpu.VMEM((max(mates - 1, 1), own, 3, dh, fwh), SENT),
            pltpu.VMEM((own, 3, dh, fwh), F32),
            pltpu.VMEM((GROUPS - 1, own, 3, dh, fwh), SENT),
            pltpu.VMEM((8, rows), F32),
            pltpu.VMEM((max(nh - 1, 1), 8, rows), F32),
            dma((2 * hd,)), dma((2 * hd,)),
            dma((own * 3,)), dma((own * 3,)),
            dma((max(mates - 1, 1), own * 3)), dma((max(mates - 1, 1), own * 3)),
            dma(((GROUPS - 1) * mates, own * 3)), dma((GROUPS - 1, own * 3)),
            dma((GROUPS, own * 3)), dma((GROUPS, own * 3)),
            dma((max(nh - 1, 1),)), dma((max(nh - 1, 1),)),
        ],
        compiler_params=pltpu.CompilerParams(
            collective_id=0, has_side_effects=True, vmem_limit_bytes=56 * 1024 * 1024
        ),
    )(
        queries, key_rows, values, gate_init, up_init, down_init,
        out_gain.reshape(1, width), step_size, head_scale,
    )
    return (scaled * out_gain[None, :]).astype(BF)


def solution(mesh):
    in_specs = (
        P("frame", "head"),
        P("frame", "head"),
        P("frame", "head"),
        P("head", None, None),
        P("head", None, None),
        P("head", None, None),
        P("head"),
        P("head"),
        P("head"),
    )
    return jax.shard_map(
        shards, mesh=mesh, in_specs=in_specs, out_specs=P("frame", "head"), check_vma=False
    )
```

time: 200 us -> 38.1 us (0.19)
  the two profiles are of different devices: /device:TPU:0 before, /device:TPU:25 now
where the time goes in v1:
time: 38.1 us; the launch traced here: 37.9 us
  Pallas kernels  36.1 us (95%)
  other arithmetic  1.78 us (5%)
    pallas_call x1, Pallas kernels, shards(): pl.pallas_call(functools.partial(kernel, (frames, nh, hd)), out_shape=jax...  36.1 us
    convert_element_type x1, other arithmetic, shards(): return (scaled * out_gain[None, :]).astype(BF)  1.78 us

profile of v1, /device:TPU:25, one launch (start us, length us, event | category | flops | bytes accessed | tf_op | source)
XLA Modules:
  0.0 37.9 jit_solution(11312339406754355489)
XLA Ops:
  0.0 0.0 copy-start
  0.0 36.1 %shard_map.91 = f32[512,256]{1,0:T(8,128)} custom-call(bf16[512,256]{1,0:T(8,128)(2,1)} %q_any.1, bf16[512,256]{1,0:T(8,128)(2,1)} %k_any.1, bf16[512,256]{1,0:T(8,128)(2,1)} %v_any.1, f32[2,128,128]{2,1,0:T(8,128)} %gate_any.1, f32[2,128,128]{2,1,0:T(8,128)} %up_any.1, f32[2,128,128]{2,1,0:T(8,128)} %down_any.1, f32[1,256]{1,0:T(1,128)} %bitcast.1, ...), custom_call_target="tpu_custom_call" | custom-call | tf_op jit(solution)/shard_map/pallas_call | solution.py:469
  36.1 0.0 copy-done
  36.1 1.8 %multiply_convert_fusion = bf16[512,256]{1,0:T(8,128)(2,1)} fusion(f32[512,256]{1,0:T(8,128)} %shard_map.91, f32[256]{0:T(256)S(1)} %copy-done), kind=kLoop, calls=%fused_computation | loop fusion | flops 262144 | bytes 787456 | tf_op jit(solution)/shard_map/convert_element_type | solution.py:517
Async XLA Ops:
  0.0 36.1 %copy-start = (f32[256]{0:T(256)S(1)}, f32[256]{0:T(256)}, u32[]{:S(2)}) copy-start(f32[256]{0:T(256)} %param.17) | copy-start | bytes 3076
